TPU v7x, 32 devices: a whole 2x2x4 slice. The times are simulated.
32 devices in a mesh: fsdp: 4 (over z), ctx: 4 (over x, core), tp: 2 (over y).
Axes of the slice: x: 2, y: 2, z: 4, core: 2. Of those that a mesh axis runs over, the one named last changes fastest.
Arguments:
- x_in: bfloat16 [8, 1024, 2048], P(None, ('fsdp', 'ctx')), may hold values from -6 to 6
- cotangent: bfloat16 [8, 1024, 2048], P(None, ('fsdp', 'ctx')), may hold values from -6 to 6
- lengths: int32 [8], replicated, may hold values from 128 to 1024, as said below
- adapter_ids: int32 [8], replicated, may hold values from 0 to 7
- w_qkv: bfloat16 [3, 2048, 2048], P(None, 'fsdp', 'tp'), may hold values from -0.125 to 0.125
- w_out: bfloat16 [2048, 2048], P('tp', 'fsdp'), may hold values from -2 to 2
- w_up: bfloat16 [2048, 8192], P('fsdp', 'tp'), may hold values from -0.125 to 0.125
- w_down: bfloat16 [8192, 2048], P('tp', 'fsdp'), may hold values from -0.0625 to 0.0625
- ln_gain: float32 [2, 2048], replicated, may hold values from 0.1 to 1.9
- ln_bias: float32 [2, 2048], replicated, may hold values from -1.5 to 1.5
- a_qkv: bfloat16 [3, 2048, 128], replicated, may hold values from -0.125 to 0.125
- b_qkv: bfloat16 [3, 128, 2048], P(None, None, 'tp'), may hold values from -0.5 to 0.5
- a_out: bfloat16 [2048, 128], P('tp'), may hold values from -2 to 2
- b_out: bfloat16 [128, 2048], replicated, may hold values from -0.5 to 0.5
- a_up: bfloat16 [2048, 128], replicated, may hold values from -0.125 to 0.125
- b_up: bfloat16 [128, 8192], P(None, 'tp'), may hold values from -0.5 to 0.5
- a_down: bfloat16 [8192, 128], P('tp'), may hold values from -0.0625 to 0.0625
- b_down: bfloat16 [128, 2048], replicated, may hold values from -0.5 to 0.5
Outputs:
- activations: bfloat16 [8, 1024, 2048], P(None, ('fsdp', 'ctx'))
- input_grad: bfloat16 [8, 1024, 2048], P(None, ('fsdp', 'ctx'))
- grad_a_qkv: float32 [3, 2048, 128], replicated
- grad_b_qkv: float32 [3, 128, 2048], P(None, None, 'tp')
- grad_a_out: float32 [2048, 128], P('tp')
- grad_b_out: float32 [128, 2048], replicated
- grad_a_up: float32 [2048, 128], replicated
- grad_b_up: float32 [128, 8192], P(None, 'tp')
- grad_a_down: float32 [8192, 128], P('tp')
- grad_b_down: float32 [128, 2048], replicated
Inputs may be any that keep to these rules, and one draw needn't show every extreme that they name: `lengths`: each aligned block of 2 sequences holds at least one sequence of length 1024.
All inputs are finite; a program needn't handle non-finite values.
Results may differ from a plain program's by a relative error of at most 0.019.
Values may be sent and summed in bfloat16 or wider, within the bound.
A program may use at most 256 MiB of HBM per device.

v0:
```python
from functools import partial
import math
import jax
import jax.numpy as jnp
from jax import lax
from jax.sharding import PartitionSpec as P

HEAD_DIM = 128
RANK = 16
ADAPTERS = 8
NORM_EPS = 1e-06
GELU_COEF = 0.7978845608028654


def norm_rows(values, gain_row, shift_row):
    center = values - jnp.mean(values, axis=-1, keepdims=True)
    spread = jnp.mean(center * center, axis=-1, keepdims=True)
    return center * lax.rsqrt(spread + NORM_EPS) * gain_row + shift_row


def gelu_tanh(values):
    return (
        0.5 * values * (1.0 + jnp.tanh(GELU_COEF * (values + 0.044715 * values * values * values)))
    )


def product(left_side, right_side):
    return jnp.dot(left_side, right_side, preferred_element_type=jnp.float32)


def against(left_side, right_side):
    return lax.dot_general(
        left_side, right_side, (((1,), (1,)), ((), ())), preferred_element_type=jnp.float32
    )


def across(left_side, right_side):
    return lax.dot_general(
        left_side, right_side, (((0,), (0,)), ((), ())), preferred_element_type=jnp.float32
    )


def local(
    x_in,
    cotangent,
    lengths,
    adapter_ids,
    w_qkv,
    w_out,
    w_up,
    w_down,
    ln_gain,
    ln_bias,
    a_qkv,
    b_qkv,
    a_out,
    b_out,
    a_up,
    b_up,
    a_down,
    b_down,
):
    n_ctx = lax.axis_size("ctx")
    n_fsdp = lax.axis_size("fsdp")
    owner_index = lax.axis_index("fsdp")
    seq_total, piece_rows, model_width = x_in.shape
    per_dev = seq_total // n_fsdp
    local_len = n_fsdp * piece_rows
    dev_rows = per_dev * local_len
    key_count = n_ctx * local_len
    heads_width = w_qkv.shape[2]
    heads_here = heads_width // HEAD_DIM
    score_scale = 1.0 / math.sqrt(HEAD_DIM)
    dealt_x, dealt_cot = (
        lax.all_to_all(x_in, "fsdp", split_axis=0, concat_axis=1, tiled=True),
        lax.all_to_all(cotangent, "fsdp", split_axis=0, concat_axis=1, tiled=True),
    )
    x_rows = dealt_x.reshape(dev_rows, model_width)
    my_lengths = lax.dynamic_slice_in_dim(lengths, owner_index * per_dev, per_dev)
    my_ids = lax.dynamic_slice_in_dim(adapter_ids, owner_index * per_dev, per_dev)
    picked = (my_ids[:, None] == jnp.arange(ADAPTERS)[None, :]).astype(jnp.float32)
    pick_rows = jnp.repeat(jnp.repeat(picked, RANK, axis=1), local_len, axis=0)
    key_index = jnp.arange(key_count)
    ctx_block = key_index // local_len
    remain = key_index % local_len
    key_pos = (remain // piece_rows * n_ctx + ctx_block) * piece_rows + remain % piece_rows
    usable = key_pos[None, :] < my_lengths[:, None]
    qkv_full, out_full = (
        lax.all_gather(w_qkv, "fsdp", axis=1, tiled=True),
        lax.all_gather(w_out, "fsdp", axis=1, tiled=True),
    )
    adapt_qkv = [
        (product(x_rows, a_qkv[proj_index]) * pick_rows).astype(jnp.bfloat16)
        for proj_index in range(3)
    ]
    projected = [
        (product(x_rows, qkv_full[proj_index]) + product(adapt_qkv[proj_index], b_qkv[proj_index]))
        .astype(jnp.bfloat16)
        .reshape(per_dev, local_len, heads_width)
        for proj_index in range(3)
    ]
    queries_all = projected[0]
    keys_all, values_all = (
        lax.all_gather(projected[1], "ctx", axis=1, tiled=True),
        lax.all_gather(projected[2], "ctx", axis=1, tiled=True),
    )

    def score_block(query_heads, key_heads, usable_row):
        scores = (
            jnp.einsum("qhd,khd->hqk", query_heads, key_heads, preferred_element_type=jnp.float32)
            * score_scale
        )
        return jnp.where(usable_row[None, None, :], scores, -1e30)

    def attend(packed):
        queries, keys_seq, values_seq, usable_row = packed
        query_heads = queries.reshape(local_len, heads_here, HEAD_DIM)
        key_heads = keys_seq.reshape(key_count, heads_here, HEAD_DIM)
        value_heads = values_seq.reshape(key_count, heads_here, HEAD_DIM)
        scores = score_block(query_heads, key_heads, usable_row)
        row_max = jnp.max(scores, axis=-1, keepdims=True)
        row_total = jnp.sum(jnp.exp(scores - row_max), axis=-1, keepdims=True)
        log_total = row_max + jnp.log(row_total)
        attn_probs = jnp.exp(scores - log_total).astype(jnp.bfloat16)
        mixed_heads = jnp.einsum(
            "hqk,khd->qhd", attn_probs, value_heads, preferred_element_type=jnp.float32
        )
        return (mixed_heads.reshape(local_len, heads_width).astype(jnp.bfloat16), log_total[..., 0])

    context, log_totals = lax.map(attend, (queries_all, keys_all, values_all, usable))
    ctx_rows = context.reshape(dev_rows, heads_width)
    part_out = product(ctx_rows, out_full)
    part_adapt = product(ctx_rows, a_out) * pick_rows
    attn_sum, adapt_out_sum = lax.psum((part_out, part_adapt), "tp")
    adapt_out = adapt_out_sum.astype(jnp.bfloat16)
    attn_branch = attn_sum + product(adapt_out, b_out)
    hidden_one, norm_one_back = jax.vjp(
        partial(norm_rows, gain_row=ln_gain[0], shift_row=ln_bias[0]),
        x_rows.astype(jnp.float32) + attn_branch,
    )
    hidden_low = hidden_one.astype(jnp.bfloat16)
    up_full, down_full = (
        lax.all_gather(w_up, "fsdp", axis=0, tiled=True),
        lax.all_gather(w_down, "fsdp", axis=1, tiled=True),
    )
    adapt_up = (product(hidden_low, a_up) * pick_rows).astype(jnp.bfloat16)
    pre_act = product(hidden_low, up_full) + product(adapt_up, b_up)
    activated, gelu_back = jax.vjp(gelu_tanh, pre_act)
    gelu_out = activated.astype(jnp.bfloat16)
    part_down = product(gelu_out, down_full)
    part_adapt_down = product(gelu_out, a_down) * pick_rows
    down_sum, adapt_down_sum = lax.psum((part_down, part_adapt_down), "tp")
    adapt_down = adapt_down_sum.astype(jnp.bfloat16)
    second_in = hidden_one + down_sum + product(adapt_down, b_down)
    layer_out, norm_two_back = jax.vjp(
        partial(norm_rows, gain_row=ln_gain[1], shift_row=ln_bias[1]), second_in
    )
    grad_out = dealt_cot.reshape(dev_rows, model_width).astype(jnp.float32)
    (grad_second,) = norm_two_back(grad_out)
    grad_down_low = grad_second.astype(jnp.bfloat16)
    up_back, down_back = (
        lax.all_gather(w_up, "fsdp", axis=0, tiled=True),
        lax.all_gather(w_down, "fsdp", axis=1, tiled=True),
    )
    grad_adapt_down = (against(grad_down_low, b_down) * pick_rows).astype(jnp.bfloat16)
    grad_b_down = across(adapt_down, grad_down_low)
    grad_a_down = across(gelu_out, grad_adapt_down)
    grad_gelu = against(grad_down_low, down_back) + against(grad_adapt_down, a_down)
    (grad_pre,) = gelu_back(grad_gelu)
    grad_pre_low = grad_pre.astype(jnp.bfloat16)
    grad_b_up = across(adapt_up, grad_pre_low)
    part_hidden = against(grad_pre_low, up_back)
    part_adapt_up = against(grad_pre_low, b_up)
    grad_hidden_sum, grad_adapt_up_sum = lax.psum((part_hidden, part_adapt_up), "tp")
    grad_adapt_up = (grad_adapt_up_sum * pick_rows).astype(jnp.bfloat16)
    grad_a_up = across(hidden_low, grad_adapt_up)
    grad_hidden = grad_second + grad_hidden_sum + against(grad_adapt_up, a_up)
    (grad_first,) = norm_one_back(grad_hidden)
    grad_attn_low = grad_first.astype(jnp.bfloat16)
    qkv_back, out_back = (
        lax.all_gather(w_qkv, "fsdp", axis=1, tiled=True),
        lax.all_gather(w_out, "fsdp", axis=1, tiled=True),
    )
    grad_adapt_out = (against(grad_attn_low, b_out) * pick_rows).astype(jnp.bfloat16)
    grad_b_out = across(adapt_out, grad_attn_low)
    grad_a_out = across(ctx_rows, grad_adapt_out)
    grad_context = (against(grad_attn_low, out_back) + against(grad_adapt_out, a_out)).astype(
        jnp.bfloat16
    )

    def attend_back(packed):
        queries, keys_seq, values_seq, usable_row, log_total, grad_ctx_seq = packed
        query_heads = queries.reshape(local_len, heads_here, HEAD_DIM)
        key_heads = keys_seq.reshape(key_count, heads_here, HEAD_DIM)
        value_heads = values_seq.reshape(key_count, heads_here, HEAD_DIM)
        scores = score_block(query_heads, key_heads, usable_row)
        attn_probs = jnp.exp(scores - log_total[..., None])
        probs_low = attn_probs.astype(jnp.bfloat16)
        grad_heads = grad_ctx_seq.reshape(local_len, heads_here, HEAD_DIM)
        grad_values = jnp.einsum(
            "hqk,qhd->khd", probs_low, grad_heads, preferred_element_type=jnp.float32
        )
        grad_probs = jnp.einsum(
            "qhd,khd->hqk", grad_heads, value_heads, preferred_element_type=jnp.float32
        )
        row_dot = jnp.sum(attn_probs * grad_probs, axis=-1, keepdims=True)
        grad_scores = (attn_probs * (grad_probs - row_dot)).astype(jnp.bfloat16)
        grad_query = (
            jnp.einsum("hqk,khd->qhd", grad_scores, key_heads, preferred_element_type=jnp.float32)
            * score_scale
        )
        grad_keys = (
            jnp.einsum("hqk,qhd->khd", grad_scores, query_heads, preferred_element_type=jnp.float32)
            * score_scale
        )
        return (
            grad_query.reshape(local_len, heads_width).astype(jnp.bfloat16),
            grad_keys.reshape(key_count, heads_width),
            grad_values.reshape(key_count, heads_width),
        )

    grad_ctx_seqs = grad_context.reshape(per_dev, local_len, heads_width)
    grad_queries, grad_keys_all, grad_values_all = lax.map(
        attend_back, (queries_all, keys_all, values_all, usable, log_totals, grad_ctx_seqs)
    )
    grad_keys_mine, grad_values_mine = (
        lax.psum_scatter(
            grad_keys_all.astype(jnp.bfloat16), "ctx", scatter_dimension=1, tiled=True
        ).astype(jnp.float32),
        lax.psum_scatter(
            grad_values_all.astype(jnp.bfloat16), "ctx", scatter_dimension=1, tiled=True
        ).astype(jnp.float32),
    )
    grad_proj = [
        grad_queries.reshape(dev_rows, heads_width),
        grad_keys_mine.astype(jnp.bfloat16).reshape(dev_rows, heads_width),
        grad_values_mine.astype(jnp.bfloat16).reshape(dev_rows, heads_width),
    ]
    grad_b_qkv = jnp.stack(
        [across(adapt_qkv[proj_index], grad_proj[proj_index]) for proj_index in range(3)]
    )
    part_input = (
        against(grad_proj[0], qkv_back[0])
        + against(grad_proj[1], qkv_back[1])
        + against(grad_proj[2], qkv_back[2])
    )
    part_adapt_qkv = jnp.stack(
        [against(grad_proj[proj_index], b_qkv[proj_index]) for proj_index in range(3)]
    )
    grad_input_sum, grad_adapt_qkv_sum = (
        lax.psum(part_input.astype(jnp.bfloat16), "tp").astype(jnp.float32),
        lax.psum(part_adapt_qkv.astype(jnp.bfloat16), "tp").astype(jnp.float32),
    )
    grad_adapt_qkv = (grad_adapt_qkv_sum * pick_rows[None]).astype(jnp.bfloat16)
    grad_a_qkv = jnp.stack([across(x_rows, grad_adapt_qkv[proj_index]) for proj_index in range(3)])
    grad_input = (
        grad_first
        + grad_input_sum
        + against(grad_adapt_qkv[0], a_qkv[0])
        + against(grad_adapt_qkv[1], a_qkv[1])
        + against(grad_adapt_qkv[2], a_qkv[2])
    )
    summed_grads = lax.psum(
        (
            grad_a_qkv,
            grad_b_qkv,
            grad_a_out,
            grad_b_out,
            grad_a_up,
            grad_b_up,
            grad_a_down,
            grad_b_down,
        ),
        ("fsdp", "ctx"),
    )
    out_low = layer_out.astype(jnp.bfloat16).reshape(per_dev, local_len, model_width)
    input_low = grad_input.astype(jnp.bfloat16).reshape(per_dev, local_len, model_width)
    back_out, back_input = (
        lax.all_to_all(out_low, "fsdp", split_axis=1, concat_axis=0, tiled=True),
        lax.all_to_all(input_low, "fsdp", split_axis=1, concat_axis=0, tiled=True),
    )
    return (
        back_out,
        back_input,
        summed_grads[0],
        summed_grads[1],
        summed_grads[2],
        summed_grads[3],
        summed_grads[4],
        summed_grads[5],
        summed_grads[6],
        summed_grads[7],
    )


def solution(mesh):
    return jax.shard_map(
        local,
        mesh=mesh,
        in_specs=(
            P(None, ("fsdp", "ctx"), None),
            P(None, ("fsdp", "ctx"), None),
            P(),
            P(),
            P(None, "fsdp", "tp"),
            P("tp", "fsdp"),
            P("fsdp", "tp"),
            P("tp", "fsdp"),
            P(),
            P(),
            P(),
            P(None, None, "tp"),
            P("tp", None),
            P(),
            P(),
            P(None, "tp"),
            P("tp", None),
            P(),
        ),
        out_specs=(
            P(None, ("fsdp", "ctx"), None),
            P(None, ("fsdp", "ctx"), None),
            P(),
            P(None, None, "tp"),
            P("tp", None),
            P(),
            P(),
            P(None, "tp"),
            P("tp", None),
            P(),
        ),
        check_vma=False,
    )
```

profile of v0, /device:TPU:0, one launch (start us, length us, event | category | flops | bytes accessed | tf_op | source)
XLA Modules:
  0.0 2011.4 jit_solution(7236679362293835580)
XLA Ops:
  14.6 104.2 %all-to-all-done = bf16[8,64,2048]{2,1,0:T(8,128)(2,1)S(1)} async-done(((bf16[8,64,2048]{2,1,0:T(8,128)(2,1)}), bf16[8,64,2048]{2,1,0:T(8,128)(2,1)S(1)}, u32[]{:S(2)}, u32[]{:S(2)}) %all-to-all-start) | async-done | bytes 2097184 | tf_op jit(solution)/shard_map/all_to_all | solution.py:75
  124.0 141.4 %all-gather.7.cloned.1.call-done = bf16[3,2048,1024]{2,1,0:T(8,128)(2,1)} async-done(((bf16[3,512,1024]{2,1,0:T(8,128)(2,1)}), bf16[3,2048,1024]{2,1,0:T(8,128)(2,1)}) %all-gather.7.cloned.1.call-update) | async-done | bytes 12582928 | tf_op jit(solution)/shard_map/all_gather | solution.py:89
  297.6 11.3 all-gather.11.cloned.1.call-done
  308.8 37.2 %all-gather.9.cloned.1.call-done = bf16[2,1024,1024]{1,2,0:T(8,128)(2,1)} async-done(((bf16[2,256,1024]{1,2,0:T(8,128)(2,1)}), bf16[2,1024,1024]{1,2,0:T(8,128)(2,1)}) %all-gather.9.cloned.1.call-update) | async-done | bytes 4194320 | tf_op jit(solution)/shard_map/all_gather | solution.py:105
  347.1 26.9 %while.26 = (s32[]{:T(128)}, bf16[2,256,1024]{2,1,0:T(8,128)(2,1)}, f32[2,8,256]{2,1,0:T(8,128)S(1)}, bf16[2,1024,1024]{1,2,0:T(8,128)(2,1)}, pred[2,1024]{1,0:T...) while((s32[]{:T(128)}, bf16[2,256,1024]{2,1,0:T(8,128)(2,1)}, ...), condition=%wide.region_3.4_spmd, body=%wide.region_0.3_spmd.sunk | while | flops 1097070592 | bytes 46208640 | solution.py:130
  374.1 54.2 %all-gather.13.cloned.1.call-done = bf16[1024,2048]{1,0:T(8,128)(2,1)} async-done(((bf16[1024,512]{1,0:T(8,128)(2,1)}), bf16[1024,2048]{1,0:T(8,128)(2,1)}) %all-gather.13.cloned.1.call-update) | async-done | bytes 4194320 | tf_op jit(solution)/shard_map/all_gather | solution.py:90
  439.0 19.6 all-reduce.20
  458.6 88.7 %all-reduce.11.cloned.1.call-done = f32[512,2048]{1,0:T(8,128)} async-done(((f32[512,2048]{1,0:T(8,128)}), f32[512,2048]{1,0:T(8,128)}) %all-reduce.11.cloned.1.call-update) | async-done | bytes 4194320 | tf_op jit(solution)/shard_map/psum | solution.py:134
  559.5 276.1 %all-gather.15.cloned.1.call-done = bf16[2048,4096]{1,0:T(8,128)(2,1)} async-done(((bf16[512,4096]{1,0:T(8,128)(2,1)}), bf16[2048,4096]{1,0:T(8,128)(2,1)}) %all-gather.15.cloned.1.call-update) | async-done | bytes 16777232 | tf_op jit(solution)/shard_map/all_gather | solution.py:143
  835.6 20.4 %multiply_convert_fusion.1 = (bf16[512,4096]{1,0:T(8,128)(2,1)}, f32[512,4096]{1,0:T(8,128)}) fusion(f32[512,4096]{1,0:T(8,128)} %fusion.102, bf16[512,2048]{1,0:T(8,128)(2,1)S(1)} %fusion.31, bf16[2048,4096]{1,0:T(8,128)(2,1)} %all-gather.15.cloned.1.call-done), kind=kOutput, calls=%fused_computation.52 | convolution fusion | flops 8610906112 | bytes 39845888 | tf_op jit(solution)/shard_map/dot_general | solution.py:28
  856.0 266.2 %all-gather.17.cloned.1.call-done = bf16[4096,2048]{1,0:T(8,128)(2,1)} async-done(((bf16[4096,512]{1,0:T(8,128)(2,1)}), bf16[4096,2048]{1,0:T(8,128)(2,1)}) %all-gather.17.cloned.1.call-update) | async-done | bytes 16777232 | tf_op jit(solution)/shard_map/all_gather | solution.py:144
  1122.2 14.9 fusion.103
  1138.7 51.1 %all_to_all.60 = bf16[8,64,2048]{2,1,0:T(8,128)(2,1)S(1)} all-to-all(bf16[8,64,2048]{2,1,0:T(8,128)(2,1)S(1)} %copy-done.39), channel_id=1, replica_groups=mesh['fsdp'=4,'ctx'=4,'tp'=2] {'fsdp'}, dimensions={0} | all-to-all | bytes 4194304 | tf_op jit(solution)/shard_map/all_to_all | solution.py:76
  1194.8 18.6 all-reduce.21
  1213.4 35.5 %all-reduce.13.cloned.1.call-done = f32[512,2048]{1,0:T(8,128)} async-done(((f32[512,2048]{1,0:T(8,128)}), f32[512,2048]{1,0:T(8,128)}) %all-reduce.13.cloned.1.call-update) | async-done | bytes 4194320 | tf_op jit(solution)/shard_map/psum | solution.py:152
  1264.7 22.3 %fusion.22 = bf16[512,4096]{1,0:T(8,128)(2,1)} fusion(f32[512,4096]{1,0:T(8,128)} %get-tuple-element.250, f32[512,4096]{1,0:T(8,128)} %fusion.104, bf16[512,2048]{1,0:T(8,128)(2,1)S(1)} %add_convert_fusion.4, bf16[4096,2048]{1,0:T(8,128)(2,1)} %all-gather.17.cloned.1.call-done), kind=kOutput, calls=%fused_computation.49 | convolution fusion | flops 8642363392 | bytes 39845888 | tf_op jit(solution)/shard_map/dot_general | solution.py:32
  1291.3 14.0 fusion.105
  1305.4 113.3 %all-reduce.17.cloned.1.call-done = (f32[512,2048]{1,0:T(8,128)}, f32[512,128]{1,0:T(8,128)}) async-done(((f32[512,2048]{1,0:T(8,128)}, f32[512,128]{1,0:T(8,128)}), (f32[512,2048]{1,0:T(8,128)}, f32[512,128]{1,0:T(8,128)})) %all-reduce.17.cloned.1.call-update) | async-done | bytes 4456464 | tf_op jit(solution)/shard_map/psum | solution.py:174
  1436.4 91.7 %while.27 = (s32[]{:T(128)}, bf16[2,256,1024]{2,1,0:T(8,128)(2,1)}, bf16[2,1024,1024]{2,1,0:T(8,128)(2,1)}, bf16[2,1024,1024]{2,1,0:T(8,128)(2,1)}, bf16[2,1024,...) while((s32[]{:T(128)}, bf16[2,256,1024]{2,1,0:T(8,128)(2,1)}, ...), condition=%wide.region_20.21_spmd, body=%wide.region_18.20_spmd.sunk | while | flops 2718431232 | bytes 173603120 | solution.py:223
  1545.5 27.2 %reduce-scatter.3.cloned.1.call-done = bf16[2,256,1024]{2,1,0:T(8,128)(2,1)} async-done(((bf16[2,1024,1024]{2,1,0:T(8,128)(2,1)}), bf16[2,256,1024]{2,1,0:T(8,128)(2,1)}) %reduce-scatter.3.cloned.1.call-update) | async-done | bytes 1048592 | tf_op jit(solution)/shard_map/reduce_scatter | solution.py:227
  1574.4 45.4 %reduce-scatter.5.cloned.1.call-done = bf16[2,256,1024]{2,1,0:T(8,128)(2,1)} async-done(((bf16[2,1024,1024]{2,1,0:T(8,128)(2,1)}), bf16[2,256,1024]{2,1,0:T(8,128)(2,1)}) %reduce-scatter.5.cloned.1.call-update) | async-done | bytes 1048592 | tf_op jit(solution)/shard_map/reduce_scatter | solution.py:230
  1649.0 56.3 %all-reduce.19.cloned.1.call-done = (bf16[3,512,128]{2,1,0:T(8,128)(2,1)}, bf16[512,2048]{1,0:T(8,128)(2,1)}) async-done(((bf16[3,512,128]{2,1,0:T(8,128)(2,1)}, bf16[512,2048]{1,0:T(8,128)(2,1)}), (bf16[3,512,128]{2,1,0:T(8,128)(2,1)}, bf16[512,2048]{1,0:T(8,128)(2,1)})) %all-reduce.19.cloned.1.call-update) | async-done | bytes 2490384 | tf_op jit(solution)/shard_map/psum | solution.py:252
  1727.2 67.8 %all-to-all-done.3 = bf16[2,256,2048]{2,0,1:T(2,128)(2,1)S(1)} async-done(((bf16[2,256,2048]{2,0,1:T(2,128)(2,1)}), bf16[2,256,2048]{2,0,1:T(2,128)(2,1)S(1)}, u32[]{:S(2)}, u32[]{:S(2)}) %all-to-all-start.3) | async-done | bytes 2097184 | tf_op jit(solution)/shard_map/all_to_all | solution.py:280
  1797.2 196.3 %all-reduce.15.cloned.1.call-done = (f32[3,2048,128]{1,2,0:T(8,128)}, f32[3,128,1024]{2,1,0:T(8,128)}, f32[1024,128]{1,0:T(8,128)}, f32[128,2048]{1,0:T(8,128)},...) async-done(((f32[3,2048,128]{1,2,0:T(8,128)}, f32[3,128,1024]{2,1,0:T(8,128)}, f32[1024,128]{1,0:T(8,128)}, ...) | async-done | bytes 12582928 | tf_op jit(solution)/shard_map/psum | solution.py:263
  (365 shorter events, 313.9 us)
Async XLA Ops:
  7.2 1185.3 %copy-start = (bf16[4096,128]{1,0:T(8,128)(2,1)S(1)}, bf16[4096,128]{1,0:T(8,128)(2,1)}, u32[]{:S(2)}) copy-start(bf16[4096,128]{1,0:T(8,128)(2,1)} %param.38) | copy-start | bytes 3145732
  7.2 258.2 %all-gather.7.cloned.1.call-start = ((), (), s32[]{:S(2)}) async-start(), calls=%async_computation.6 | async-start | bytes 15728640 | tf_op jit(solution)/shard_map/all_gather | solution.py:89
  7.9 110.8 %all-to-all-start = ((bf16[8,64,2048]{2,1,0:T(8,128)(2,1)}), bf16[8,64,2048]{2,1,0:T(8,128)(2,1)S(1)}, u32[]{:S(2)}, u32[]{:S(2)}) async-start(bf16[8,64,2048]{2,1,0:T(8,128)(2,1)} %param.22), calls=%async_computation | async-start | bytes 4194304 | tf_op jit(solution)/shard_map/all_to_all | solution.py:75
  14.3 294.6 %all-gather.11.cloned.1.call-start = ((), (), s32[]{:S(2)}) async-start(), calls=%async_computation.8 | async-start | bytes 5242880 | tf_op jit(solution)/shard_map/all_gather | solution.py:104
  14.6 1413.2 %copy-start.71 = (f32[2,128]{1,0:T(2,128)}, f32[2,128]{1,0:T(2,128)S(1)}, u32[]{:S(2)}) copy-start(f32[2,128]{1,0:T(2,128)S(1)} %reshape.257) | copy-start | bytes 3076
  121.8 425.5 %copy-start.6 = (bf16[4,2,64,2048]{3,2,0,1:T(8,128)(2,1)}, bf16[4,2,64,2048]{3,2,0,1:T(8,128)(2,1)S(1)}, u32[]{:S(2)}) copy-start(bf16[4,2,64,2048]{3,2,0,1:T(8,128)(2,1)S(1)} %copy.63) | copy-start | bytes 6291460
  124.0 145.9 %copy-start.53 = (bf16[512,128]{1,0:T(8,128)(2,1)}, bf16[512,128]{1,0:T(8,128)(2,1)S(1)}, u32[]{:S(2)}) copy-start(bf16[512,128]{1,0:T(8,128)(2,1)S(1)} %fusion.34) | copy-start | bytes 393220
  274.5 71.5 %all-gather.9.cloned.1.call-start = ((), (), s32[]{:S(2)}) async-start(), calls=%async_computation.7 | async-start | bytes 5242880 | tf_op jit(solution)/shard_map/all_gather | solution.py:105
  285.6 142.6 %all-gather.13.cloned.1.call-start = ((), (), s32[]{:S(2)}) async-start(), calls=%async_computation.9 | async-start | bytes 5242880 | tf_op jit(solution)/shard_map/all_gather | solution.py:90
  286.2 261.1 %all-reduce.11.cloned.1.call-start = ((), (), s32[]{:S(2)}) async-start(), calls=%async_computation.10 | async-start | bytes 8388608 | tf_op jit(solution)/shard_map/psum | solution.py:134
  374.1 61.0 %copy-start.73 = (f32[2,8,256]{2,1,0:T(8,128)}, f32[2,8,256]{2,1,0:T(8,128)S(1)}, u32[]{:S(2)}) copy-start(f32[2,8,256]{2,1,0:T(8,128)S(1)} %get-tuple-element.410) | copy-start | bytes 49156
  435.1 400.5 %all-gather.15.cloned.1.call-start = ((), (), s32[]{:S(2)}) async-start(), calls=%async_computation.11 | async-start | bytes 20971520 | tf_op jit(solution)/shard_map/all_gather | solution.py:143
  435.7 686.5 %all-gather.17.cloned.1.call-start = ((), (), s32[]{:S(2)}) async-start(), calls=%async_computation.12 | async-start | bytes 20971520 | tf_op jit(solution)/shard_map/all_gather | solution.py:144
  436.5 812.5 %all-reduce.13.cloned.1.call-start = ((), (), s32[]{:S(2)}) async-start(), calls=%async_computation.13 | async-start | bytes 8388608 | tf_op jit(solution)/shard_map/psum | solution.py:152
  458.6 91.9 %copy-start.47 = (bf16[512,128]{1,0:T(8,128)(2,1)}, bf16[512,128]{1,0:T(8,128)(2,1)S(1)}, u32[]{:S(2)}) copy-start(bf16[512,128]{1,0:T(8,128)(2,1)S(1)} %all-reduce.20) | copy-start | bytes 393220
  552.5 283.1 %copy-start.14 = (bf16[512,2048]{1,0:T(8,128)(2,1)}, bf16[512,2048]{1,0:T(8,128)(2,1)S(1)}, u32[]{:S(2)}) copy-start(bf16[512,2048]{1,0:T(8,128)(2,1)S(1)} %fusion.31) | copy-start | bytes 6291460
  1137.1 281.6 %all-reduce.17.cloned.1.call-start = ((), (), s32[]{:S(2)}) async-start(), calls=%async_computation.17 | async-start | bytes 8912896 | tf_op jit(solution)/shard_map/psum | solution.py:174
  1305.3 114.4 %copy-start.37 = (bf16[2048,128]{1,0:T(8,128)(2,1)S(1)}, bf16[2048,128]{1,0:T(8,128)(2,1)}, u32[]{:S(2)}) copy-start(bf16[2048,128]{1,0:T(8,128)(2,1)} %param.36) | copy-start | bytes 1572868
  1305.3 267.4 %reduce-scatter.3.cloned.1.call-start = ((), (), s32[]{:S(2)}) async-start(), calls=%async_computation.14 | async-start | bytes 5242880 | tf_op jit(solution)/shard_map/reduce_scatter | solution.py:227
  1528.1 91.7 %reduce-scatter.5.cloned.1.call-start = ((), (), s32[]{:S(2)}) async-start(), calls=%async_computation.15 | async-start | bytes 5242880 | tf_op jit(solution)/shard_map/reduce_scatter | solution.py:230
  1533.2 185.6 %all-to-all-start.1 = ((bf16[2,256,2048]{2,0,1:T(2,128)(2,1)}), bf16[2,256,2048]{2,0,1:T(2,128)(2,1)}, u32[]{:S(2)}, u32[]{:S(2)}) async-start(bf16[2,256,2048]{2,0,1:T(2,128)(2,1)} %copy.68), calls=%async_computation.1 | async-start | bytes 4194304 | tf_op jit(solution)/shard_map/all_to_all | solution.py:279
  1537.9 167.4 %all-reduce.19.cloned.1.call-start = ((), (), s32[]{:S(2)}) async-start(), calls=%async_computation.18 | async-start | bytes 4980736 | tf_op jit(solution)/shard_map/psum | solution.py:252
  1633.4 360.0 %all-reduce.15.cloned.1.call-start = ((), (), s32[]{:S(2)}) async-start(), calls=%async_computation.16 | async-start | bytes 25165824 | tf_op jit(solution)/shard_map/psum | solution.py:263
  1718.7 76.3 %all-to-all-start.3 = ((bf16[2,256,2048]{2,0,1:T(2,128)(2,1)}), bf16[2,256,2048]{2,0,1:T(2,128)(2,1)S(1)}, u32[]{:S(2)}, u32[]{:S(2)}) async-start(bf16[2,256,2048]{2,0,1:T(2,128)(2,1)} %copy.76), calls=%async_computation.5 | async-start | bytes 4194304 | tf_op jit(solution)/shard_map/all_to_all | solution.py:280
  (84 other events, 574.5 us)
Sparse Core Ops, SparseCore 0:
  9.6 255.7 all-gather.6
  274.7 34.1 all-gather.10
  311.0 35.0 all-gather.8
  347.5 80.7 all-gather.12
  435.2 112.0 all-reduce.10
  548.8 286.7 all-gather.14
  837.2 284.9 all-gather.16
  1137.2 111.6 all-reduce.12
  1305.5 113.2 all-reduce.16
  1528.2 44.4 reduce-scatter.2
  1575.3 44.4 reduce-scatter.4
  1633.6 71.6 all-reduce.18
  1711.8 281.6 all-reduce.14
where the time goes:
time: 2020 us; the launch traced here: 2010 us
  waiting for transfers between devices  1520 us (75%)
  matrix products  235 us (12%)
  local copies, waits for them, and re-layouts  108 us (5%)
  blocking collectives  89.4 us (4%)
  other arithmetic  22 us (1%)
    all_gather x1, waiting for transfers between devices, local(): lax.all_gather(w_up, 'fsdp', axis=0, tiled=True)  276 us
    all_gather x1, waiting for transfers between devices, local(): lax.all_gather(w_down, 'fsdp', axis=1, tiled=True)  266 us
    psum x1, waiting for transfers between devices, local(): lax.psum((grad_a_qkv, grad_b_qkv, grad_a_out, grad_b_out, grad_a_up, grad...  196 us
    all_gather x1, waiting for transfers between devices, local(): lax.all_gather(w_qkv, 'fsdp', axis=1, tiled=True)  141 us
    psum x1, waiting for transfers between devices, local(): lax.psum((part_hidden, part_adapt_up), 'tp')  113 us
    all_to_all x1, waiting for transfers between devices, local(): lax.all_to_all(x_in, 'fsdp', split_axis=0, concat_axis=1, tiled=True)  104 us
    psum x1, waiting for transfers between devices, local(): attn_sum, adapt_out_sum = lax.psum((part_out, part_adapt), 'tp')  88.7 us
    dot_general x18, matrix products, product(): return jnp.dot(left_side, right_side, preferred_element_type=jnp.float32)  86.5 us
  transfers between devices with their start and end apart: 16, of which 15 were waited for; matrix products, arithmetic and copies ran while one was open for 7% of the time, Pallas kernels for 0%

commit v1 on v0

--- a/solution.py
+++ b/solution.py
@@ -261,17 +261,20 @@
         + against(grad_adapt_qkv[2], a_qkv[2])
     )
     summed_grads = lax.psum(
-        (
-            grad_a_qkv,
-            grad_b_qkv,
-            grad_a_out,
-            grad_b_out,
-            grad_a_up,
-            grad_b_up,
-            grad_a_down,
-            grad_b_down,
+        lax.psum(
+            (
+                grad_a_qkv,
+                grad_b_qkv,
+                grad_a_out,
+                grad_b_out,
+                grad_a_up,
+                grad_b_up,
+                grad_a_down,
+                grad_b_down,
+            ),
+            "ctx",
         ),
-        ("fsdp", "ctx"),
+        "fsdp",
     )
     out_low = layer_out.astype(jnp.bfloat16).reshape(per_dev, local_len, model_width)
     input_low = grad_input.astype(jnp.bfloat16).reshape(per_dev, local_len, model_width)

time: 2020 us -> 2480 us (1.23)
  waiting for transfers between devices: 1520 us -> 1990 us
    psum x0 -> x1, waiting for transfers between devices: none -> 304 us  [local(): lax.psum(lax.psum((grad_a_qkv, grad_b_qkv, grad_a_out, grad_b_out, grad_a...]
    all_to_all x1, waiting for transfers between devices: 0.01 us -> 94.4 us  [local(): lax.all_to_all(out_low, 'fsdp', split_axis=1, concat_axis=0, tiled=True)]
    all_to_all x1, waiting for transfers between devices: 67.8 us -> 95.2 us  [local(): lax.all_to_all(input_low, 'fsdp', split_axis=1, concat_axis=0, tiled=True)]
    psum x1, waiting for transfers between devices: 196 us -> 223 us  [local(): lax.psum((grad_a_qkv, grad_b_qkv, grad_a_out, grad_b_out, grad_a_up, grad...]
  transfers between devices with their start and end apart: 16 -> 17, of which waited for: 15 -> 17; matrix products, arithmetic and copies ran while one was open for 7% -> 5% of each run, Pallas kernels for 0% -> 0%
where the time goes in v1:
time: 2480 us; the launch traced here: 2470 us
  waiting for transfers between devices  1990 us (80%)
  matrix products  239 us (10%)
  local copies, waits for them, and re-layouts  106 us (4%)
  blocking collectives  89.4 us (4%)
    psum x1, waiting for transfers between devices, local(): lax.psum(lax.psum((grad_a_qkv, grad_b_qkv, grad_a_out, grad_b_out, grad_a...  304 us
    all_gather x1, waiting for transfers between devices, local(): lax.all_gather(w_up, 'fsdp', axis=0, tiled=True)  276 us
    all_gather x1, waiting for transfers between devices, local(): lax.all_gather(w_down, 'fsdp', axis=1, tiled=True)  266 us
    psum x1, waiting for transfers between devices, local(): lax.psum((grad_a_qkv, grad_b_qkv, grad_a_out, grad_b_out, grad_a_up, grad...  223 us
    all_gather x1, waiting for transfers between devices, local(): lax.all_gather(w_qkv, 'fsdp', axis=1, tiled=True)  141 us
    psum x1, waiting for transfers between devices, local(): lax.psum((part_hidden, part_adapt_up), 'tp')  113 us
    all_to_all x1, waiting for transfers between devices, local(): lax.all_to_all(x_in, 'fsdp', split_axis=0, concat_axis=1, tiled=True)  104 us
    all_to_all x1, waiting for transfers between devices, local(): lax.all_to_all(input_low, 'fsdp', split_axis=1, concat_axis=0, tiled=True)  95.2 us
  transfers between devices with their start and end apart: 17, of which 17 were waited for; matrix products, arithmetic and copies ran while one was open for 5% of the time, Pallas kernels for 0%

profile of v1, /device:TPU:0, one launch (start us, length us, event | category | flops | bytes accessed | tf_op | source)
XLA Modules:
  0.0 2474.7 jit_solution(9039997213035784807)
XLA Ops:
  14.6 104.2 %all-to-all-done = bf16[8,64,2048]{2,1,0:T(8,128)(2,1)S(1)} async-done(((bf16[8,64,2048]{2,1,0:T(8,128)(2,1)}), bf16[8,64,2048]{2,1,0:T(8,128)(2,1)S(1)}, u32[]{:S(2)}, u32[]{:S(2)}) %all-to-all-start) | async-done | bytes 2097184 | tf_op jit(solution)/shard_map/all_to_all | solution.py:75
  124.0 141.4 %all-gather.7.cloned.1.call-done = bf16[3,2048,1024]{2,1,0:T(8,128)(2,1)} async-done(((bf16[3,512,1024]{2,1,0:T(8,128)(2,1)}), bf16[3,2048,1024]{2,1,0:T(8,128)(2,1)}) %all-gather.7.cloned.1.call-update) | async-done | bytes 12582928 | tf_op jit(solution)/shard_map/all_gather | solution.py:89
  308.8 37.2 %all-gather.9.cloned.1.call-done = bf16[2,1024,1024]{1,2,0:T(8,128)(2,1)} async-done(((bf16[2,256,1024]{1,2,0:T(8,128)(2,1)}), bf16[2,1024,1024]{1,2,0:T(8,128)(2,1)}) %all-gather.9.cloned.1.call-update) | async-done | bytes 4194320 | tf_op jit(solution)/shard_map/all_gather | solution.py:105
  347.1 26.9 %while.26 = (s32[]{:T(128)}, bf16[2,256,1024]{2,1,0:T(8,128)(2,1)}, f32[2,8,256]{2,1,0:T(8,128)S(1)}, bf16[2,1024,1024]{1,2,0:T(8,128)(2,1)}, pred[2,1024]{1,0:T...) while((s32[]{:T(128)}, bf16[2,256,1024]{2,1,0:T(8,128)(2,1)}, ...), condition=%wide.region_3.4_spmd, body=%wide.region_0.3_spmd.sunk | while | flops 1097070592 | bytes 46208640 | solution.py:130
  374.1 54.2 %all-gather.13.cloned.1.call-done = bf16[1024,2048]{1,0:T(8,128)(2,1)} async-done(((bf16[1024,512]{1,0:T(8,128)(2,1)}), bf16[1024,2048]{1,0:T(8,128)(2,1)}) %all-gather.13.cloned.1.call-update) | async-done | bytes 4194320 | tf_op jit(solution)/shard_map/all_gather | solution.py:90
  439.0 19.6 all-reduce.24
  458.6 88.7 %all-reduce.13.cloned.1.call-done = f32[512,2048]{1,0:T(8,128)} async-done(((f32[512,2048]{1,0:T(8,128)}), f32[512,2048]{1,0:T(8,128)}) %all-reduce.13.cloned.1.call-update) | async-done | bytes 4194320 | tf_op jit(solution)/shard_map/psum | solution.py:134
  559.5 276.1 %all-gather.15.cloned.1.call-done = bf16[2048,4096]{1,0:T(8,128)(2,1)} async-done(((bf16[512,4096]{1,0:T(8,128)(2,1)}), bf16[2048,4096]{1,0:T(8,128)(2,1)}) %all-gather.15.cloned.1.call-update) | async-done | bytes 16777232 | tf_op jit(solution)/shard_map/all_gather | solution.py:143
  835.6 20.4 multiply_convert_fusion.1
  856.0 266.2 %all-gather.17.cloned.1.call-done = bf16[4096,2048]{1,0:T(8,128)(2,1)} async-done(((bf16[4096,512]{1,0:T(8,128)(2,1)}), bf16[4096,2048]{1,0:T(8,128)(2,1)}) %all-gather.17.cloned.1.call-update) | async-done | bytes 16777232 | tf_op jit(solution)/shard_map/all_gather | solution.py:144
  1122.2 15.0 fusion.103
  1138.8 51.1 %all_to_all.60 = bf16[8,64,2048]{2,1,0:T(8,128)(2,1)S(1)} all-to-all(bf16[8,64,2048]{2,1,0:T(8,128)(2,1)S(1)} %copy-done.38), channel_id=1, replica_groups=mesh['fsdp'=4,'ctx'=4,'tp'=2] {'fsdp'}, dimensions={0} | all-to-all | bytes 4194304 | tf_op jit(solution)/shard_map/all_to_all | solution.py:76
  1194.9 18.6 all-reduce.25
  1213.5 35.5 %all-reduce.15.cloned.1.call-done = f32[512,2048]{1,0:T(8,128)} async-done(((f32[512,2048]{1,0:T(8,128)}), f32[512,2048]{1,0:T(8,128)}) %all-reduce.15.cloned.1.call-update) | async-done | bytes 4194320 | tf_op jit(solution)/shard_map/psum | solution.py:152
  1264.9 22.3 fusion.22
  1305.7 113.3 %all-reduce.21.cloned.1.call-done = (f32[512,2048]{1,0:T(8,128)}, f32[512,128]{1,0:T(8,128)}) async-done(((f32[512,2048]{1,0:T(8,128)}, f32[512,128]{1,0:T(8,128)}), (f32[512,2048]{1,0:T(8,128)}, f32[512,128]{1,0:T(8,128)})) %all-reduce.21.cloned.1.call-update) | async-done | bytes 4456464 | tf_op jit(solution)/shard_map/psum | solution.py:174
  1436.7 91.3 %while.27 = (s32[]{:T(128)}, bf16[2,256,1024]{2,1,0:T(8,128)(2,1)}, bf16[2,1024,1024]{2,1,0:T(8,128)(2,1)}, bf16[2,1024,1024]{2,1,0:T(8,128)(2,1)}, bf16[2,1024,...) while((s32[]{:T(128)}, bf16[2,256,1024]{2,1,0:T(8,128)(2,1)}, ...), condition=%wide.region_20.21_spmd, body=%wide.region_18.20_spmd.sunk | while | flops 2718431232 | bytes 173603120 | solution.py:223
  1536.6 36.0 %reduce-scatter.3.cloned.1.call-done = bf16[2,256,1024]{2,1,0:T(8,128)(2,1)} async-done(((bf16[2,1024,1024]{2,1,0:T(8,128)(2,1)}), bf16[2,256,1024]{2,1,0:T(8,128)(2,1)}) %reduce-scatter.3.cloned.1.call-update) | async-done | bytes 1048592 | tf_op jit(solution)/shard_map/reduce_scatter | solution.py:227
  1574.3 45.4 %reduce-scatter.5.cloned.1.call-done = bf16[2,256,1024]{2,1,0:T(8,128)(2,1)} async-done(((bf16[2,1024,1024]{2,1,0:T(8,128)(2,1)}), bf16[2,256,1024]{2,1,0:T(8,128)(2,1)}) %reduce-scatter.5.cloned.1.call-update) | async-done | bytes 1048592 | tf_op jit(solution)/shard_map/reduce_scatter | solution.py:230
  1649.2 55.9 %all-reduce.23.cloned.1.call-done = (bf16[3,512,128]{2,1,0:T(8,128)(2,1)}, bf16[512,2048]{1,0:T(8,128)(2,1)}) async-done(((bf16[3,512,128]{2,1,0:T(8,128)(2,1)}, bf16[512,2048]{1,0:T(8,128)(2,1)}), (bf16[3,512,128]{2,1,0:T(8,128)(2,1)}, bf16[512,2048]{1,0:T(8,128)(2,1)})) %all-reduce.23.cloned.1.call-update) | async-done | bytes 2490384 | tf_op jit(solution)/shard_map/psum | solution.py:252
  1709.7 223.3 %all-reduce.17.cloned.1.call-done = (f32[3,2048,128]{1,2,0:T(8,128)}, f32[3,128,1024]{2,1,0:T(8,128)}, f32[1024,128]{1,0:T(8,128)}, f32[128,2048]{1,0:T(8,128)},...) async-done(((f32[3,2048,128]{1,2,0:T(8,128)}, f32[3,128,1024]{2,1,0:T(8,128)}, f32[1024,128]{1,0:T(8,128)}, ...) | async-done | bytes 12582928 | tf_op jit(solution)/shard_map/psum | solution.py:264
  1952.6 94.4 %all-to-all-done.1 = bf16[2,256,2048]{2,0,1:T(2,128)(2,1)S(1)} async-done(((bf16[2,256,2048]{2,0,1:T(2,128)(2,1)}), bf16[2,256,2048]{2,0,1:T(2,128)(2,1)S(1)}, u32[]{:S(2)}, u32[]{:S(2)}) %all-to-all-start.1) | async-done | bytes 2097184 | tf_op jit(solution)/shard_map/all_to_all | solution.py:282
  2054.0 95.2 %all-to-all-done.3 = bf16[2,256,2048]{2,0,1:T(2,128)(2,1)} async-done(((bf16[2,256,2048]{2,0,1:T(2,128)(2,1)}), bf16[2,256,2048]{2,0,1:T(2,128)(2,1)}, u32[]{:S(2)}, u32[]{:S(2)}) %all-to-all-start.3) | async-done | bytes 2097184 | tf_op jit(solution)/shard_map/all_to_all | solution.py:283
  2152.9 303.9 %all-reduce.19.cloned.1.call-done = (f32[3,2048,128]{1,2,0:T(8,128)}, f32[3,128,1024]{2,1,0:T(8,128)}, f32[1024,128]{1,0:T(8,128)}, f32[128,2048]{1,0:T(8,128)},...) async-done(((f32[3,2048,128]{1,2,0:T(8,128)}, f32[3,128,1024]{2,1,0:T(8,128)}, f32[1024,128]{1,0:T(8,128)}, ...) | async-done | bytes 12582928 | tf_op jit(solution)/shard_map/psum | solution.py:263
  (366 shorter events, 341.2 us)
Async XLA Ops:
  7.2 1185.4 %copy-start = (bf16[4096,128]{1,0:T(8,128)(2,1)S(1)}, bf16[4096,128]{1,0:T(8,128)(2,1)}, u32[]{:S(2)}) copy-start(bf16[4096,128]{1,0:T(8,128)(2,1)} %param.38) | copy-start | bytes 3145732
  7.2 258.2 %all-gather.7.cloned.1.call-start = ((), (), s32[]{:S(2)}) async-start(), calls=%async_computation.6 | async-start | bytes 15728640 | tf_op jit(solution)/shard_map/all_gather | solution.py:89
  7.9 110.8 %all-to-all-start = ((bf16[8,64,2048]{2,1,0:T(8,128)(2,1)}), bf16[8,64,2048]{2,1,0:T(8,128)(2,1)S(1)}, u32[]{:S(2)}, u32[]{:S(2)}) async-start(bf16[8,64,2048]{2,1,0:T(8,128)(2,1)} %param.22), calls=%async_computation | async-start | bytes 4194304 | tf_op jit(solution)/shard_map/all_to_all | solution.py:75
  14.3 294.6 %all-gather.11.cloned.1.call-start = ((), (), s32[]{:S(2)}) async-start(), calls=%async_computation.8 | async-start | bytes 5242880 | tf_op jit(solution)/shard_map/all_gather | solution.py:104
  14.6 1413.5 %copy-start.70 = (f32[2,128]{1,0:T(2,128)}, f32[2,128]{1,0:T(2,128)S(1)}, u32[]{:S(2)}) copy-start(f32[2,128]{1,0:T(2,128)S(1)} %reshape.257) | copy-start | bytes 3076
  121.8 425.5 %copy-start.6 = (bf16[4,2,64,2048]{3,2,0,1:T(8,128)(2,1)}, bf16[4,2,64,2048]{3,2,0,1:T(8,128)(2,1)S(1)}, u32[]{:S(2)}) copy-start(bf16[4,2,64,2048]{3,2,0,1:T(8,128)(2,1)S(1)} %copy.63) | copy-start | bytes 6291460
  124.0 145.9 %copy-start.52 = (bf16[512,128]{1,0:T(8,128)(2,1)}, bf16[512,128]{1,0:T(8,128)(2,1)S(1)}, u32[]{:S(2)}) copy-start(bf16[512,128]{1,0:T(8,128)(2,1)S(1)} %fusion.34) | copy-start | bytes 393220
  274.5 71.5 %all-gather.9.cloned.1.call-start = ((), (), s32[]{:S(2)}) async-start(), calls=%async_computation.7 | async-start | bytes 5242880 | tf_op jit(solution)/shard_map/all_gather | solution.py:105
  285.6 142.6 %all-gather.13.cloned.1.call-start = ((), (), s32[]{:S(2)}) async-start(), calls=%async_computation.9 | async-start | bytes 5242880 | tf_op jit(solution)/shard_map/all_gather | solution.py:90
  286.2 261.1 %all-reduce.13.cloned.1.call-start = ((), (), s32[]{:S(2)}) async-start(), calls=%async_computation.10 | async-start | bytes 8388608 | tf_op jit(solution)/shard_map/psum | solution.py:134
  435.1 400.5 %all-gather.15.cloned.1.call-start = ((), (), s32[]{:S(2)}) async-start(), calls=%async_computation.11 | async-start | bytes 20971520 | tf_op jit(solution)/shard_map/all_gather | solution.py:143
  435.7 686.5 %all-gather.17.cloned.1.call-start = ((), (), s32[]{:S(2)}) async-start(), calls=%async_computation.12 | async-start | bytes 20971520 | tf_op jit(solution)/shard_map/all_gather | solution.py:144
  436.5 812.6 %all-reduce.15.cloned.1.call-start = ((), (), s32[]{:S(2)}) async-start(), calls=%async_computation.13 | async-start | bytes 8388608 | tf_op jit(solution)/shard_map/psum | solution.py:152
  458.6 91.9 %copy-start.46 = (bf16[512,128]{1,0:T(8,128)(2,1)}, bf16[512,128]{1,0:T(8,128)(2,1)S(1)}, u32[]{:S(2)}) copy-start(bf16[512,128]{1,0:T(8,128)(2,1)S(1)} %all-reduce.24) | copy-start | bytes 393220
  552.5 283.1 %copy-start.14 = (bf16[512,2048]{1,0:T(8,128)(2,1)}, bf16[512,2048]{1,0:T(8,128)(2,1)S(1)}, u32[]{:S(2)}) copy-start(bf16[512,2048]{1,0:T(8,128)(2,1)S(1)} %fusion.31) | copy-start | bytes 6291460
  1137.2 281.7 %all-reduce.21.cloned.1.call-start = ((), (), s32[]{:S(2)}) async-start(), calls=%async_computation.18 | async-start | bytes 8912896 | tf_op jit(solution)/shard_map/psum | solution.py:174
  1305.6 114.4 %copy-start.36 = (bf16[2048,128]{1,0:T(8,128)(2,1)S(1)}, bf16[2048,128]{1,0:T(8,128)(2,1)}, u32[]{:S(2)}) copy-start(bf16[2048,128]{1,0:T(8,128)(2,1)} %param.36) | copy-start | bytes 1572868
  1305.6 267.0 %reduce-scatter.3.cloned.1.call-start = ((), (), s32[]{:S(2)}) async-start(), calls=%async_computation.14 | async-start | bytes 5242880 | tf_op jit(solution)/shard_map/reduce_scatter | solution.py:227
  1528.0 91.7 %reduce-scatter.5.cloned.1.call-start = ((), (), s32[]{:S(2)}) async-start(), calls=%async_computation.15 | async-start | bytes 5242880 | tf_op jit(solution)/shard_map/reduce_scatter | solution.py:230
  1528.7 176.4 %all-reduce.23.cloned.1.call-start = ((), (), s32[]{:S(2)}) async-start(), calls=%async_computation.19 | async-start | bytes 4980736 | tf_op jit(solution)/shard_map/psum | solution.py:252
  1633.3 299.6 %all-reduce.17.cloned.1.call-start = ((), (), s32[]{:S(2)}) async-start(), calls=%async_computation.16 | async-start | bytes 25165824 | tf_op jit(solution)/shard_map/psum | solution.py:264
  1709.6 747.2 %all-reduce.19.cloned.1.call-start = ((), (), s32[]{:S(2)}) async-start(), calls=%async_computation.17 | async-start | bytes 25165824 | tf_op jit(solution)/shard_map/psum | solution.py:263
  1938.0 109.0 %all-to-all-start.1 = ((bf16[2,256,2048]{2,0,1:T(2,128)(2,1)}), bf16[2,256,2048]{2,0,1:T(2,128)(2,1)S(1)}, u32[]{:S(2)}, u32[]{:S(2)}) async-start(bf16[2,256,2048]{2,0,1:T(2,128)(2,1)} %copy.68), calls=%async_computation.1 | async-start | bytes 4194304 | tf_op jit(solution)/shard_map/all_to_all | solution.py:282
  2047.0 102.1 %all-to-all-start.3 = ((bf16[2,256,2048]{2,0,1:T(2,128)(2,1)}), bf16[2,256,2048]{2,0,1:T(2,128)(2,1)}, u32[]{:S(2)}, u32[]{:S(2)}) async-start(bf16[2,256,2048]{2,0,1:T(2,128)(2,1)} %copy.76), calls=%async_computation.5 | async-start | bytes 4194304 | tf_op jit(solution)/shard_map/all_to_all | solution.py:283
  (84 other events, 626.9 us)
Sparse Core Ops, SparseCore 0:
  9.6 255.7 all-gather.6
  274.7 34.1 all-gather.10
  311.0 35.0 all-gather.8
  347.5 80.7 all-gather.12
  435.2 112.0 all-reduce.12
  548.8 286.7 all-gather.14
  837.2 284.9 all-gather.16
  1137.4 111.6 all-reduce.14
  1305.7 113.2 all-reduce.20
  1528.1 44.4 reduce-scatter.2
  1575.2 44.4 reduce-scatter.4
  1633.4 71.6 all-reduce.22
  1709.7 223.1 all-reduce.16
  1936.2 520.5 all-reduce.18
